TPU v7x, 128 devices: a whole 4x4x4 slice. The times are simulated.
128 devices in a mesh: gy: 8 (over z_lo, x), gz: 16 (over y, z_hi, core).
Axes of the slice: x: 4, y: 4, z: 4 (z_hi: 2, z_lo: 2; z = z_hi * 2 + z_lo), core: 2. Of those that a mesh axis runs over, the one named last changes fastest.
Arguments:
- density: float32 [1024, 128, 256], P('gy', 'gz'), may hold values from 0.5 to 2
- momentum: float32 [3, 1024, 128, 256], P(None, 'gy', 'gz'), may hold values from -3 to 3
- energy: float32 [1024, 128, 256], P('gy', 'gz'), may hold values from 2 to 4
- wall_operator: float32 [1024, 1024], replicated, may hold values from -0.1875 to 0.1875
- span_operator: float32 [128, 128], replicated, may hold values from -0.5 to 0.5
- damping: float32 [1024], replicated, may hold values from 0.1 to 1
Outputs:
- new_density: float32 [1024, 128, 256], P('gy', 'gz')
- new_momentum: float32 [3, 1024, 128, 256], P(None, 'gy', 'gz')
- new_energy: float32 [1024, 128, 256], P('gy', 'gz')
All inputs are finite; a program needn't handle non-finite values.
Results may differ from a plain program's by a relative error of at most 0.00009.
Values sent between devices are 32-bit elements; how exact they have to be, the bound alone decides.
A program may use at most 256 MiB of HBM per device.

v0:
```python
import jax
import jax.numpy as jnp
from jax import lax
from jax.sharding import PartitionSpec as P

gamma_less = 0.4
time_step = 0.1


def with_halo(cells, sides, width, closed):
    for axis, dim in sides:
        count = lax.axis_size(axis)
        ends = count if closed else count - 1
        head = lax.slice_in_dim(cells, 0, width, axis=dim)
        tail = lax.slice_in_dim(cells, cells.shape[dim] - width, cells.shape[dim], axis=dim)
        cells = jnp.concatenate(
            [
                lax.ppermute(tail, axis, [(i, (i + 1) % count) for i in range(ends)]),
                cells,
                lax.ppermute(head, axis, [((i + 1) % count, i) for i in range(ends)]),
            ],
            axis=dim,
        )
    return cells


def flux_along(conserved, direction):
    velocity = conserved[1 + direction] / conserved[0]
    kinetic = (
        0.5
        * (conserved[1] * conserved[1] + conserved[2] * conserved[2] + conserved[3] * conserved[3])
        / conserved[0]
    )
    pressure = gamma_less * (conserved[4] - kinetic)
    components = [conserved[1 + direction]]
    for column in range(3):
        product = conserved[1 + column] * velocity
        if column == direction:
            product = product + pressure
        components.append(product)
    components.append((conserved[4] + pressure) * velocity)
    return jnp.stack(components)


def x_derivative(flux_field):
    widths = [(0, 0)] * (flux_field.ndim - 1) + [(2, 2)]
    padded = jnp.pad(flux_field, widths, mode="edge")
    return (
        8.0 * (padded[..., 3:-1] - padded[..., 1:-3]) - (padded[..., 4:] - padded[..., :-4])
    ) / 12.0


def fourth_difference(padded, along_axis, length_out):

    def shifted(offset):
        return lax.slice_in_dim(padded, offset, offset + length_out, axis=along_axis)

    return shifted(0) - 4.0 * shifted(1) + 6.0 * shifted(2) - 4.0 * shifted(3) + shifted(4)


def local(density, momentum, energy, wall_operator, span_operator, damping):
    conserved = jnp.concatenate([density[None], momentum, energy[None]], axis=0)
    rows_here = conserved.shape[1]
    planes_here = conserved.shape[2]
    first_row = lax.axis_index("gy") * rows_here
    local_damping = lax.dynamic_slice_in_dim(damping, first_row, rows_here)
    along_x = x_derivative(flux_along(conserved, 0))
    upward = flux_along(conserved, 1)
    sideways = flux_along(conserved, 2)
    derivative = jnp.einsum(
        "ij,fjzx->fizx",
        wall_operator,
        lax.all_to_all(upward, "gy", split_axis=3, concat_axis=1, tiled=True),
        precision=lax.Precision.HIGHEST,
    )
    deriv_y = lax.all_to_all(derivative, "gy", split_axis=1, concat_axis=3, tiled=True)
    derivative = jnp.einsum(
        "ij,fyjx->fyix",
        span_operator,
        lax.all_to_all(sideways, "gz", split_axis=3, concat_axis=2, tiled=True),
        precision=lax.Precision.HIGHEST,
    )
    deriv_z = lax.all_to_all(derivative, "gz", split_axis=2, concat_axis=3, tiled=True)
    near_y = with_halo(conserved, (("gy", 1),), 2, False)
    near_z = with_halo(conserved, (("gz", 2),), 2, True)
    smoothing = fourth_difference(near_y, 1, rows_here) + fourth_difference(near_z, 2, planes_here)
    tendency = -along_x - deriv_y - deriv_z - local_damping[None, :, None, None] * smoothing
    advanced = conserved + time_step * tendency
    return (advanced[0], advanced[1:4], advanced[4])


def solution(mesh):
    in_specs = (P("gy", "gz", None), P(None, "gy", "gz", None), P("gy", "gz", None), P(), P(), P())
    out_specs = (P("gy", "gz", None), P(None, "gy", "gz", None), P("gy", "gz", None))
    return jax.shard_map(local, mesh=mesh, in_specs=in_specs, out_specs=out_specs, check_vma=False)
```

profile of v0, /device:TPU:87, one launch (start us, length us, event | category | flops | bytes accessed | tf_op | source)
XLA Modules:
  0.0 498.6 jit_solution(11741611885511762760)
XLA Ops:
  29.7 71.1 %all-to-all-done = f32[5,128,8,256]{1,2,0,3:T(8,128)} async-done(((f32[5,128,8,256]{1,2,0,3:T(8,128)}), f32[5,128,8,256]{1,2,0,3:T(8,128)}, u32[]{:S(2)}, u32[]{:S(2)}) %all-to-all-start) | async-done | bytes 5242912 | tf_op jit(solution)/shard_map/all_to_all | solution.py:73
  100.8 8.7 %all-to-all-start.2 = ((f32[5,128,8,256]{1,2,0,3:T(8,128)}), f32[5,128,8,256]{1,2,0,3:T(8,128)}, u32[]{:S(2)}, u32[]{:S(2)}) async-start(f32[5,128,8,256]{1,2,0,3:T(8,128)} %copy.89), calls=%async_computation.2 | async-start | bytes 10485760 | tf_op jit(solution)/shard_map/all_to_all | solution.py:80
  109.5 7.9 %copy.83 = f32[5,8,128,8,32]{2,1,4,3,0:T(8,128)} copy(f32[5,8,128,8,32]{2,3,0,4,1:T(8,128)} %bitcast.17) | data formatting | bytes 10485760 | tf_op jit(solution)/shard_map/all_to_all | solution.py:73
  117.4 6.8 %all_to_all.55 = f32[5,1024,8,32]{1,3,2,0:T(8,128)} reshape(f32[5,8,128,8,32]{2,1,4,3,0:T(8,128)} %copy.83) | data formatting | bytes 10485760 | tf_op jit(solution)/shard_map/all_to_all | solution.py:73
  124.2 22.0 %fusion.25 = f32[5,1024,8,32]{1,3,2,0:T(8,128)} fusion(f32[5,1024,8,32]{1,3,2,0:T(8,128)} %all_to_all.55, f32[1024,1024]{1,0:T(8,128)} %param.9), kind=kOutput, calls=%fused_computation.42 | convolution fusion | flops 16106127360 | bytes 14680064 | tf_op jit(solution)/shard_map/ij,fjzx->fizx/dot_general | solution.py:70
  146.1 13.3 %copy.84 = f32[5,1024,8,32]{3,2,0,1:T(8,128)} copy(f32[5,1024,8,32]{1,3,2,0:T(8,128)} %fusion.25) | data formatting | bytes 10485760 | tf_op jit(solution)/shard_map/ij,fjzx->fizx/transpose | solution.py:70
  159.4 14.8 %reshape.21 = f32[8,1,163840]{2,1,0:T(1,128)} reshape(f32[1024,5,8,32]{3,2,1,0:T(8,128)} %bitcast.138) | data formatting | bytes 10485760
  174.2 15.9 %all-to-all-done.2 = f32[5,128,8,256]{1,2,0,3:T(8,128)} async-done(((f32[5,128,8,256]{1,2,0,3:T(8,128)}), f32[5,128,8,256]{1,2,0,3:T(8,128)}, u32[]{:S(2)}, u32[]{:S(2)}) %all-to-all-start.2) | async-done | bytes 5242912 | tf_op jit(solution)/shard_map/all_to_all | solution.py:80
  190.1 16.9 %all-to-all-start.1 = ((f32[8,1,163840]{2,1,0:T(1,128)}), f32[8,1,163840]{2,1,0:T(1,128)}, u32[]{:S(2)}, u32[]{:S(2)}) async-start(f32[8,1,163840]{2,1,0:T(1,128)} %reshape.21), calls=%async_computation.1 | async-start | bytes 10485760 | tf_op jit(solution)/shard_map/all_to_all | solution.py:76
  210.7 11.4 %fusion.28 = f32[5,128,128,16]{2,1,3,0:T(8,128)} fusion(f32[5,128,128,16]{1,3,2,0:T(8,128)S(1)} %bitcast.150, f32[128,128]{1,0:T(8,128)S(1)} %copy-done), kind=kOutput, calls=%fused_computation.43 | convolution fusion | flops 2013265920 | bytes 10551296 | tf_op jit(solution)/shard_map/ij,fyjx->fyix/dot_general | solution.py:77
  222.1 6.1 %copy.93 = f32[5,128,128,16]{1,3,0,2:T(8,128)} copy(f32[5,128,128,16]{2,1,3,0:T(8,128)} %fusion.28) | data formatting | bytes 10485760 | tf_op jit(solution)/shard_map/ij,fyjx->fyix/transpose | solution.py:77
  228.2 56.2 %all-to-all-done.1 = f32[8,1,163840]{2,1,0:T(1,128)} async-done(((f32[8,1,163840]{2,1,0:T(1,128)}), f32[8,1,163840]{2,1,0:T(1,128)}, u32[]{:S(2)}, u32[]{:S(2)}) %all-to-all-start.1) | async-done | bytes 5242912 | tf_op jit(solution)/shard_map/all_to_all | solution.py:76
  284.4 8.1 %all-to-all-start.3 = ((f32[5,128,128,16]{1,3,0,2:T(8,128)}), f32[5,128,128,16]{1,3,0,2:T(8,128)}, u32[]{:S(2)}, u32[]{:S(2)}) async-start(f32[5,128,128,16]{1,3,0,2:T(8,128)} %copy.93), calls=%async_computation.3 | async-start | bytes 10485760 | tf_op jit(solution)/shard_map/all_to_all | solution.py:83
  298.0 5.6 %fusion.42 = (f32[5,2,8,256]{1,2,3,0:T(8,128)}, f32[5,2,8,256]{1,2,3,0:T(8,128)}) fusion(f32[5,128,8,256]{1,2,3,0:T(8,128)S(1)} %pad_maximum_fusion.4), kind=kLoop, calls=%fused_computation.88 | loop fusion | bytes 327680 | tf_op jit(solution)/shard_map/slice | solution.py:15
  312.1 5.5 %collective-permute-start = (f32[5,2,8,256]{3,2,1,0:T(8,128)S(1)}, f32[5,2,8,256]{3,2,1,0:T(8,128)}, u32[]{:S(2)}, u32[]{:S(2)}) collective-permute-start(f32[5,2,8,256]{3,2,1,0:T(8,128)S(1)} %copy.97), channel_id=1, source_target_pairs={{0,16},{16,32},{32,48},{48,64},{64,80},{80,96},{96,112},{1,17},{17... | collective-permute-start | bytes 245768 | tf_op jit(solution)/shard_map/ppermute | solution.py:18
  326.1 14.6 %maximum_maximum_fusion = (f32[5,130,8,256]{1,2,3,0:T(8,128)}, f32[5,130,8,256]{1,2,3,0:T(8,128)}) fusion(f32[1,128,8,256]{1,2,3,0:T(8,128)} %bitcast.145, f32[3,128,8,256]{1,2,3,0:T(8,128)S(1)} %copy.72, f32[1,128,8,256]{1,2,3,0:T(8,128)} %bitcast.141, f32[5,2,8,256]{1,2,3,0:T(8,128)} %copy.98, f32[5,2,8,256]{1,2,3,0:T(8,128)} %copy.100), kind=kLoop, calls=%fused_computation | loop fusion | flops 7987200 | bytes 16056320 | tf_op jit(solution)/shard_map/concatenate | solution.py:16
  340.7 23.0 %collective-permute-done.2 = f32[5,128,2,256]{1,2,3,0:T(2,128)} collective-permute-done((f32[5,128,2,256]{1,2,3,0:T(2,128)}, f32[5,128,2,256]{1,2,3,0:T(2,128)}, u32[]{:S(2)}, u32[]{:S(2)}) %collective-permute-start.2) | collective-permute-done | bytes 1310752 | tf_op jit(solution)/shard_map/ppermute | solution.py:18
  363.7 24.3 %collective-permute-done.3 = f32[5,128,2,256]{1,2,3,0:T(2,128)} collective-permute-done((f32[5,128,2,256]{1,2,3,0:T(2,128)}, f32[5,128,2,256]{1,2,3,0:T(2,128)}, u32[]{:S(2)}, u32[]{:S(2)}) %collective-permute-start.3) | collective-permute-done | bytes 1310752 | tf_op jit(solution)/shard_map/ppermute | solution.py:20
  388.0 8.9 %maximum_maximum_fusion.1 = (f32[5,128,10,256]{1,2,3,0:T(8,128)}, f32[5,128,10,256]{1,2,3,0:T(8,128)}) fusion(f32[1,128,8,256]{1,2,3,0:T(8,128)S(1)} %bitcast.147, f32[3,128,8,256]{1,2,3,0:T(8,128)S(1)} %copy.72, f32[1,128,8,256]{1,2,3,0:T(8,128)S(1)} %bitcast.142, f32[5,128,2,256]{1,2,3,0:T(2,128)} %collective-permute-done.2, ...), kind=kLoop, calls=%fused_computation.2 | loop fusion | flops 9830400 | bytes 20971520 | tf_op jit(solution)/shard_map/concatenate | solution.py:16
  397.5 16.8 %reduce = f32[8,163840]{1,0:T(8,128)} reduce(f32[8,1,163840]{2,1,0:T(1,128)} %all-to-all-done.1, f32[]{:T(128)} %broadcast.28), dimensions={1}, to_apply=%all_to_all.56.reduce_sub_computation | reduce | bytes 10485764 | tf_op jit(solution)/shard_map/all_to_all | solution.py:76
  414.3 16.3 %reshape.22 = f32[1024,5,8,32]{3,2,1,0:T(8,128)} reshape(f32[8,163840]{1,0:T(8,128)} %reduce) | data formatting | bytes 10485760
  430.6 14.0 %copy.109 = f32[5,128,8,8,32]{1,2,4,3,0:T(8,128)} copy(f32[5,128,8,8,32]{4,2,0,1,3:T(8,128)} %bitcast.139) | data formatting | bytes 10485760 | tf_op jit(solution)/shard_map/all_to_all | solution.py:76
  444.6 5.6 %copy.95 = f32[5,128,8,16,16]{1,4,3,2,0:T(8,128)} copy(f32[5,128,8,16,16]{1,4,0,2,3:T(8,128)} %bitcast.39) | data formatting | bytes 10485760 | tf_op jit(solution)/shard_map/all_to_all | solution.py:83
  450.2 37.2 %fusion.10 = f32[5,128,8,256]{1,2,3,0:T(8,128)} fusion(f32[5,128,8,256]{1,2,3,0:T(8,128)} %bitcast.149, f32[5,128,8,2]{1,2,3,0:T(8,128)S(1)} %reshape.18, f32[5,128,8,256]{1,2,3,0:T(8,128)} %copy-done.7, f32[5,128,8,2]{1,2,3,0:T(8,128)S(1)} %reshape.17, f32[5,128,10,256]{1,2,3,0:T(8,128)} %get-tuple-element.27, f32[5,128,10,256]{1,2,3,0:T(8,128)} %get-tuple-element.26, ...), kind=kLoop, calls=%fused_computation.18 | loop fusion | flops 41943040 | bytes 68239872 | tf_op jit(solution)/shard_map/add | solution.py:88
  (57 shorter events, 66.4 us)
Async XLA Ops:
  0.6 210.1 %copy-start = (f32[128,128]{1,0:T(8,128)S(1)}, f32[128,128]{1,0:T(8,128)}, u32[]{:S(2)}) copy-start(f32[128,128]{1,0:T(8,128)} %param.10) | copy-start | bytes 196612
  8.6 1.8 copy-start.2
  8.6 1.8 copy-start.5
  11.9 2.3 copy-start.7
  14.2 2.3 copy-start.8
  19.2 81.6 %all-to-all-start = ((f32[5,128,8,256]{1,2,0,3:T(8,128)}), f32[5,128,8,256]{1,2,0,3:T(8,128)}, u32[]{:S(2)}, u32[]{:S(2)}) async-start(f32[5,128,8,256]{1,2,0,3:T(8,128)} %copy.81), calls=%async_computation | async-start | bytes 10485760 | tf_op jit(solution)/shard_map/all_to_all | solution.py:73
  100.8 89.3 %all-to-all-start.2 = ((f32[5,128,8,256]{1,2,0,3:T(8,128)}), f32[5,128,8,256]{1,2,0,3:T(8,128)}, u32[]{:S(2)}, u32[]{:S(2)}) async-start(f32[5,128,8,256]{1,2,0,3:T(8,128)} %copy.89), calls=%async_computation.2 | async-start | bytes 10485760 | tf_op jit(solution)/shard_map/all_to_all | solution.py:80
  190.1 94.4 %all-to-all-start.1 = ((f32[8,1,163840]{2,1,0:T(1,128)}), f32[8,1,163840]{2,1,0:T(1,128)}, u32[]{:S(2)}, u32[]{:S(2)}) async-start(f32[8,1,163840]{2,1,0:T(1,128)} %reshape.21), calls=%async_computation.1 | async-start | bytes 10485760 | tf_op jit(solution)/shard_map/all_to_all | solution.py:76
  284.4 160.1 %all-to-all-start.3 = ((f32[5,128,128,16]{1,3,0,2:T(8,128)}), f32[5,128,128,16]{1,3,0,2:T(8,128)}, u32[]{:S(2)}, u32[]{:S(2)}) async-start(f32[5,128,128,16]{1,3,0,2:T(8,128)} %copy.93), calls=%async_computation.3 | async-start | bytes 10485760 | tf_op jit(solution)/shard_map/all_to_all | solution.py:83
  296.8 66.9 %collective-permute-start.2 = (f32[5,128,2,256]{1,2,3,0:T(2,128)}, f32[5,128,2,256]{1,2,3,0:T(2,128)}, u32[]{:S(2)}, u32[]{:S(2)}) collective-permute-start(f32[5,128,2,256]{1,2,3,0:T(2,128)} %get-tuple-element.28), channel_id=1, source_target_pairs={{0,1},{1,2},{2,3},{3,4},{4,5},{5,6},{6,7},{7,8},{8,9},{9,10},{10,1... | collective-permute-start | bytes 3932168 | tf_op jit(solution)/shard_map/ppermute | solution.py:18
  297.9 90.1 %collective-permute-start.3 = (f32[5,128,2,256]{1,2,3,0:T(2,128)}, f32[5,128,2,256]{1,2,3,0:T(2,128)}, u32[]{:S(2)}, u32[]{:S(2)}) collective-permute-start(f32[5,128,2,256]{1,2,3,0:T(2,128)} %get-tuple-element.29), channel_id=1, source_target_pairs={{1,0},{2,1},{3,2},{4,3},{5,4},{6,5},{7,6},{8,7},{9,8},{10,9},{11,1... | collective-permute-start | bytes 3932168 | tf_op jit(solution)/shard_map/ppermute | solution.py:20
  306.8 16.1 %collective-permute-start.1 = (f32[5,2,8,256]{3,2,1,0:T(8,128)S(1)}, f32[5,2,8,256]{3,2,1,0:T(8,128)S(1)}, u32[]{:S(2)}, u32[]{:S(2)}) collective-permute-start(f32[5,2,8,256]{3,2,1,0:T(8,128)S(1)} %copy.99), channel_id=1, source_target_pairs={{16,0},{32,16},{48,32},{64,48},{80,64},{96,80},{112,96},{17,1},{33... | collective-permute-start | bytes 245768 | tf_op jit(solution)/shard_map/ppermute | solution.py:20
  312.1 7.0 %collective-permute-start = (f32[5,2,8,256]{3,2,1,0:T(8,128)S(1)}, f32[5,2,8,256]{3,2,1,0:T(8,128)}, u32[]{:S(2)}, u32[]{:S(2)}) collective-permute-start(f32[5,2,8,256]{3,2,1,0:T(8,128)S(1)} %copy.97), channel_id=1, source_target_pairs={{0,16},{16,32},{32,48},{48,64},{64,80},{80,96},{96,112},{1,17},{17... | collective-permute-start | bytes 245768 | tf_op jit(solution)/shard_map/ppermute | solution.py:18
  326.1 61.9 %copy-start.3 = (f32[128,8,256]{0,1,2:T(8,128)S(1)}, f32[128,8,256]{0,1,2:T(8,128)}, u32[]{:S(2)}) copy-start(f32[128,8,256]{0,1,2:T(8,128)} %copy.70) | copy-start | bytes 3145732
  326.1 61.9 %copy-start.6 = (f32[128,8,256]{0,1,2:T(8,128)S(1)}, f32[128,8,256]{0,1,2:T(8,128)}, u32[]{:S(2)}) copy-start(f32[128,8,256]{0,1,2:T(8,128)} %copy.71) | copy-start | bytes 3145732
  444.6 5.7 %copy-start.4 = (f32[128,8,256]{0,1,2:T(8,128)S(1)}, f32[128,8,256]{0,1,2:T(8,128)}, u32[]{:S(2)}) copy-start(f32[128,8,256]{0,1,2:T(8,128)} %copy.70) | copy-start | bytes 3145732
  487.5 3.2 slice-start
  490.6 7.7 %copy-start.1 = (f32[128,128]{1,0:T(8,128)S(1)}, f32[128,128]{1,0:T(8,128)}, u32[]{:S(2)}) copy-start(f32[128,128]{1,0:T(8,128)} %param.10) | copy-start | bytes 196612
where the time goes:
time: 506 us; the launch traced here: 499 us
  waiting for transfers between devices  191 us (38%)
  local copies, waits for them, and re-layouts  143 us (28%)
  other arithmetic  82.7 us (16%)
  starting transfers between devices  47.6 us (9%)
  matrix products  33.4 us (7%)
    all_to_all x1, waiting for transfers between devices, local(): lax.all_to_all(upward, 'gy', split_axis=3, concat_axis=1, tiled=True)  71.1 us
    all_to_all x1, waiting for transfers between devices, local(): lax.all_to_all(derivative, 'gy', split_axis=1, concat_axis=3, tiled=True)  56.2 us
    unnamed x27, local copies, waits for them, and re-layouts  51.3 us
    add x1, other arithmetic, local(): advanced = conserved + time_step * tendency  37.2 us
    ppermute x2, waiting for transfers between devices, with_halo(): lax.ppermute(head, axis, [((i + 1) % count, i) for i in range(ends)])  24.3 us
    concatenate x2, other arithmetic, with_halo(): jnp.concatenate([lax.ppermute(tail, axis, [(i, (i + 1) % count) for i in...  23.5 us
    ppermute x2, waiting for transfers between devices, with_halo(): lax.ppermute(tail, axis, [(i, (i + 1) % count) for i in range(ends)])  23 us
    dot_general x1, matrix products, local(): jnp.einsum('ij,fjzx->fizx', wall_operator, lax.all_to_all(upward, 'gy', s...  22 us
  transfers between devices with their start and end apart: 8, of which 5 were waited for; matrix products, arithmetic and copies ran while one was open for 36% of the time, Pallas kernels for 0%

commit v1 on v0

--- a/solution.py
+++ b/solution.py
@@ -73,7 +73,10 @@
         lax.all_to_all(upward, "gy", split_axis=3, concat_axis=1, tiled=True),
         precision=lax.Precision.HIGHEST,
     )
-    deriv_y = lax.all_to_all(derivative, "gy", split_axis=1, concat_axis=3, tiled=True)
+    size = lax.axis_size("gy")
+    parts = jnp.stack(jnp.split(derivative, size, axis=1), axis=0)
+    parts = lax.all_to_all(parts, "gy", split_axis=0, concat_axis=0)
+    deriv_y = jnp.concatenate(parts, axis=3)
     derivative = jnp.einsum(
         "ij,fyjx->fyix",
         span_operator,

time: 506 us -> 459 us (0.907)
  local copies, waits for them, and re-layouts: 143 us -> 98 us
  waiting for transfers between devices: 191 us -> 219 us
  other arithmetic: 82.7 us -> 67.3 us
  starting transfers between devices: 47.6 us -> 34.6 us
    all_to_all x1, waiting for transfers between devices: 15.9 us -> 43.4 us  [local(): lax.all_to_all(sideways, 'gz', split_axis=3, concat_axis=2, tiled=True)]
    unnamed x27 -> x32, local copies, waits for them, and re-layouts: 51.3 us -> 27.2 us
    all_to_all x1 -> x0, other arithmetic: 16.8 us -> none  [local(): lax.all_to_all(derivative, 'gy', split_axis=1, concat_axis=3, tiled=True)]
    all_to_all x2 -> x0, local copies, waits for them, and re-layouts: 14.5 us -> none  [local(): lax.all_to_all(derivative, 'gy', split_axis=1, concat_axis=3, tiled=True)]
    transpose x1 -> x0, local copies, waits for them, and re-layouts: 13.3 us -> none  [local(): jnp.einsum('ij,fjzx->fizx', wall_operator, lax.all_to_all(upward, 'gy', s...]
    all_to_all x1, starting transfers between devices: 16.9 us -> 4.77 us  [local(): parts = lax.all_to_all(parts, 'gy', split_axis=0, concat_axis=0)]
    reshape x0 -> x1, local copies, waits for them, and re-layouts: none -> 5.67 us  [local(): deriv_y = jnp.concatenate(parts, axis=3)]
  transfers between devices with their start and end apart: 8 -> 8, of which waited for: 5 -> 5; matrix products, arithmetic and copies ran while one was open for 36% -> 26% of each run, Pallas kernels for 0% -> 0%
where the time goes in v1:
time: 459 us; the launch traced here: 452 us
  waiting for transfers between devices  219 us (48%)
  local copies, waits for them, and re-layouts  98 us (21%)
  other arithmetic  67.3 us (15%)
  starting transfers between devices  34.6 us (8%)
  matrix products  32.5 us (7%)
    all_to_all x1, waiting for transfers between devices, local(): lax.all_to_all(upward, 'gy', split_axis=3, concat_axis=1, tiled=True)  71.1 us
    all_to_all x1, waiting for transfers between devices, local(): parts = lax.all_to_all(parts, 'gy', split_axis=0, concat_axis=0)  57.3 us
    all_to_all x1, waiting for transfers between devices, local(): lax.all_to_all(sideways, 'gz', split_axis=3, concat_axis=2, tiled=True)  43.4 us
    add x1, other arithmetic, local(): advanced = conserved + time_step * tendency  38.6 us
    unnamed x32, local copies, waits for them, and re-layouts  27.2 us
    ppermute x2, waiting for transfers between devices, with_halo(): lax.ppermute(head, axis, [((i + 1) % count, i) for i in range(ends)])  24.3 us
    concatenate x2, other arithmetic, with_halo(): jnp.concatenate([lax.ppermute(tail, axis, [(i, (i + 1) % count) for i in...  23.5 us
    ppermute x2, waiting for transfers between devices, with_halo(): lax.ppermute(tail, axis, [(i, (i + 1) % count) for i in range(ends)])  22.6 us
  transfers between devices with their start and end apart: 8, of which 5 were waited for; matrix products, arithmetic and copies ran while one was open for 26% of the time, Pallas kernels for 0%

profile of v1, /device:TPU:87, one launch (start us, length us, event | category | flops | bytes accessed | tf_op | source)
XLA Modules:
  0.0 452.3 jit_solution(12849946512065513995)
XLA Ops:
  19.6 5.3 %all-to-all-start = ((f32[5,128,8,256]{1,2,0,3:T(8,128)}), f32[5,128,8,256]{1,2,0,3:T(8,128)}, u32[]{:S(2)}, u32[]{:S(2)}) async-start(f32[5,128,8,256]{1,2,0,3:T(8,128)} %copy.48), calls=%async_computation | async-start | bytes 10485760 | tf_op jit(solution)/shard_map/all_to_all | solution.py:73
  24.8 5.2 %copy.54 = f32[5,128,8,256]{1,2,0,3:T(8,128)} copy(f32[5,128,8,256]{1,2,3,0:T(8,128)} %copy-done.8) | data formatting | bytes 10485760 | tf_op jit(solution)/shard_map/stack | solution.py:42
  30.0 71.1 %all-to-all-done = f32[5,128,8,256]{1,2,0,3:T(8,128)} async-done(((f32[5,128,8,256]{1,2,0,3:T(8,128)}), f32[5,128,8,256]{1,2,0,3:T(8,128)}, u32[]{:S(2)}, u32[]{:S(2)}) %all-to-all-start) | async-done | bytes 5242912 | tf_op jit(solution)/shard_map/all_to_all | solution.py:73
  101.1 8.7 %all-to-all-start.2 = ((f32[5,128,8,256]{1,2,0,3:T(8,128)}), f32[5,128,8,256]{1,2,0,3:T(8,128)}, u32[]{:S(2)}, u32[]{:S(2)}) async-start(f32[5,128,8,256]{1,2,0,3:T(8,128)} %copy.54), calls=%async_computation.2 | async-start | bytes 10485760 | tf_op jit(solution)/shard_map/all_to_all | solution.py:83
  109.8 7.8 %copy.50 = f32[5,8,128,8,32]{2,1,4,3,0:T(8,128)} copy(f32[5,8,128,8,32]{2,3,0,4,1:T(8,128)} %bitcast.17) | data formatting | bytes 10485760 | tf_op jit(solution)/shard_map/all_to_all | solution.py:73
  117.6 6.7 %all_to_all.45 = f32[5,1024,8,32]{1,3,2,0:T(8,128)} reshape(f32[5,8,128,8,32]{2,1,4,3,0:T(8,128)} %copy.50) | data formatting | bytes 10485760 | tf_op jit(solution)/shard_map/all_to_all | solution.py:73
  124.4 21.1 %fusion.25 = f32[5,1024,8,32]{1,3,2,0:T(8,128)S(1)} fusion(f32[5,1024,8,32]{1,3,2,0:T(8,128)} %all_to_all.45, f32[1024,1024]{1,0:T(8,128)} %param.9), kind=kOutput, calls=%fused_computation.42 | convolution fusion | flops 16106127360 | bytes 14680064 | tf_op jit(solution)/shard_map/ij,fjzx->fizx/dot_general | solution.py:70
  153.1 43.4 %all-to-all-done.2 = f32[5,128,8,256]{1,2,0,3:T(8,128)} async-done(((f32[5,128,8,256]{1,2,0,3:T(8,128)}), f32[5,128,8,256]{1,2,0,3:T(8,128)}, u32[]{:S(2)}, u32[]{:S(2)}) %all-to-all-start.2) | async-done | bytes 5242912 | tf_op jit(solution)/shard_map/all_to_all | solution.py:83
  196.4 4.8 %all-to-all-start.1 = ((f32[8,5,128,8,32]{2,4,3,1,0:T(8,128)}), f32[8,5,128,8,32]{2,4,3,1,0:T(8,128)}, u32[]{:S(2)}, u32[]{:S(2)}) async-start(f32[8,5,128,8,32]{2,4,3,1,0:T(8,128)} %fusion.40), calls=%async_computation.1 | async-start | bytes 10485760 | tf_op jit(solution)/shard_map/all_to_all | solution.py:78
  201.2 3.7 copy.56
  204.9 11.4 %fusion.28 = f32[5,128,128,16]{2,1,3,0:T(8,128)} fusion(f32[5,128,128,16]{1,3,2,0:T(8,128)S(1)} %bitcast.174, f32[128,128]{1,0:T(8,128)S(1)} %copy-done), kind=kOutput, calls=%fused_computation.43 | convolution fusion | flops 2013265920 | bytes 10551296 | tf_op jit(solution)/shard_map/ij,fyjx->fyix/dot_general | solution.py:80
  216.3 6.1 %copy.58 = f32[5,128,128,16]{1,3,0,2:T(8,128)} copy(f32[5,128,128,16]{2,1,3,0:T(8,128)} %fusion.28) | data formatting | bytes 10485760 | tf_op jit(solution)/shard_map/ij,fyjx->fyix/transpose | solution.py:80
  222.4 57.3 %all-to-all-done.1 = f32[8,5,128,8,32]{2,4,3,1,0:T(8,128)} async-done(((f32[8,5,128,8,32]{2,4,3,1,0:T(8,128)}), f32[8,5,128,8,32]{2,4,3,1,0:T(8,128)}, u32[]{:S(2)}, u32[]{:S(2)}) %all-to-all-start.1) | async-done | bytes 5242912 | tf_op jit(solution)/shard_map/all_to_all | solution.py:78
  279.8 7.3 %all-to-all-start.3 = ((f32[5,128,128,16]{1,3,0,2:T(8,128)}), f32[5,128,128,16]{1,3,0,2:T(8,128)}, u32[]{:S(2)}, u32[]{:S(2)}) async-start(f32[5,128,128,16]{1,3,0,2:T(8,128)} %copy.58), calls=%async_computation.3 | async-start | bytes 10485760 | tf_op jit(solution)/shard_map/all_to_all | solution.py:86
  292.4 5.7 %fusion.50 = (f32[5,2,8,256]{1,2,3,0:T(8,128)}, f32[5,2,8,256]{1,2,3,0:T(8,128)}) fusion(f32[5,128,8,256]{1,2,3,0:T(8,128)S(1)} %pad_maximum_fusion.4), kind=kLoop, calls=%fused_computation.104 | loop fusion | bytes 327680 | tf_op jit(solution)/shard_map/slice | solution.py:15
  306.9 5.5 %collective-permute-start = (f32[5,2,8,256]{3,2,1,0:T(8,128)S(1)}, f32[5,2,8,256]{3,2,1,0:T(8,128)}, u32[]{:S(2)}, u32[]{:S(2)}) collective-permute-start(f32[5,2,8,256]{3,2,1,0:T(8,128)S(1)} %copy.62), channel_id=1, source_target_pairs={{0,16},{16,32},{32,48},{48,64},{64,80},{80,96},{96,112},{1,17},{17... | collective-permute-start | bytes 245768 | tf_op jit(solution)/shard_map/ppermute | solution.py:18
  313.9 3.9 copy.63
  321.0 14.6 %maximum_maximum_fusion = (f32[5,130,8,256]{1,2,3,0:T(8,128)}, f32[5,130,8,256]{1,2,3,0:T(8,128)}) fusion(f32[1,128,8,256]{1,2,3,0:T(8,128)} %bitcast.169, f32[3,128,8,256]{1,2,3,0:T(8,128)S(1)} %copy.39, f32[1,128,8,256]{1,2,3,0:T(8,128)} %bitcast.165, f32[5,2,8,256]{1,2,3,0:T(8,128)} %copy.63, f32[5,2,8,256]{1,2,3,0:T(8,128)} %copy.65), kind=kLoop, calls=%fused_computation | loop fusion | flops 7987200 | bytes 16056320 | tf_op jit(solution)/shard_map/concatenate | solution.py:16
  335.6 22.6 %collective-permute-done.2 = f32[5,128,2,256]{1,2,3,0:T(2,128)} collective-permute-done((f32[5,128,2,256]{1,2,3,0:T(2,128)}, f32[5,128,2,256]{1,2,3,0:T(2,128)}, u32[]{:S(2)}, u32[]{:S(2)}) %collective-permute-start.2) | collective-permute-done | bytes 1310752 | tf_op jit(solution)/shard_map/ppermute | solution.py:18
  358.2 24.3 %collective-permute-done.3 = f32[5,128,2,256]{1,2,3,0:T(2,128)} collective-permute-done((f32[5,128,2,256]{1,2,3,0:T(2,128)}, f32[5,128,2,256]{1,2,3,0:T(2,128)}, u32[]{:S(2)}, u32[]{:S(2)}) %collective-permute-start.3) | collective-permute-done | bytes 1310752 | tf_op jit(solution)/shard_map/ppermute | solution.py:20
  382.5 8.9 %maximum_maximum_fusion.1 = (f32[5,128,10,256]{1,2,3,0:T(8,128)}, f32[5,128,10,256]{1,2,3,0:T(8,128)}) fusion(f32[1,128,8,256]{1,2,3,0:T(8,128)S(1)} %bitcast.171, f32[3,128,8,256]{1,2,3,0:T(8,128)S(1)} %copy.39, f32[1,128,8,256]{1,2,3,0:T(8,128)S(1)} %bitcast.166, f32[5,128,2,256]{1,2,3,0:T(2,128)} %collective-permute-done.2, ...), kind=kLoop, calls=%fused_computation.2 | loop fusion | flops 9830400 | bytes 20971520 | tf_op jit(solution)/shard_map/concatenate | solution.py:16
  391.4 5.7 %copy.51 = f32[5,128,8,8,32]{1,4,3,2,0:T(8,128)} copy(f32[5,128,8,8,32]{1,4,2,0,3:T(8,128)} %bitcast.29) | data formatting | bytes 10485760 | tf_op jit(solution)/shard_map/reshape | solution.py:79
  397.1 5.6 %copy.60 = f32[5,128,8,16,16]{1,4,3,2,0:T(8,128)} copy(f32[5,128,8,16,16]{1,4,0,2,3:T(8,128)} %bitcast.44) | data formatting | bytes 10485760 | tf_op jit(solution)/shard_map/all_to_all | solution.py:86
  402.7 38.6 %fusion.10 = f32[5,128,8,256]{1,2,3,0:T(8,128)} fusion(f32[5,128,8,2]{1,2,3,0:T(8,128)S(1)} %reshape.24, f32[5,128,8,256]{1,2,3,0:T(8,128)} %copy-done.7, f32[5,128,8,2]{1,2,3,0:T(8,128)S(1)} %reshape.23, f32[5,128,10,256]{1,2,3,0:T(8,128)} %get-tuple-element.24, f32[5,128,10,256]{1,2,3,0:T(8,128)} %get-tuple-element.23, ...), kind=kLoop, calls=%fused_computation.18 | loop fusion | flops 41943040 | bytes 68239872 | tf_op jit(solution)/shard_map/add | solution.py:91
  (59 shorter events, 56.1 us)
Async XLA Ops:
  0.6 204.3 %copy-start = (f32[128,128]{1,0:T(8,128)S(1)}, f32[128,128]{1,0:T(8,128)}, u32[]{:S(2)}) copy-start(f32[128,128]{1,0:T(8,128)} %param.10) | copy-start | bytes 196612
  8.5 1.7 copy-start.2
  8.5 1.8 copy-start.5
  12.2 2.4 copy-start.7
  14.6 2.4 copy-start.8
  19.6 81.6 %all-to-all-start = ((f32[5,128,8,256]{1,2,0,3:T(8,128)}), f32[5,128,8,256]{1,2,0,3:T(8,128)}, u32[]{:S(2)}, u32[]{:S(2)}) async-start(f32[5,128,8,256]{1,2,0,3:T(8,128)} %copy.48), calls=%async_computation | async-start | bytes 10485760 | tf_op jit(solution)/shard_map/all_to_all | solution.py:73
  101.1 95.3 %all-to-all-start.2 = ((f32[5,128,8,256]{1,2,0,3:T(8,128)}), f32[5,128,8,256]{1,2,0,3:T(8,128)}, u32[]{:S(2)}, u32[]{:S(2)}) async-start(f32[5,128,8,256]{1,2,0,3:T(8,128)} %copy.54), calls=%async_computation.2 | async-start | bytes 10485760 | tf_op jit(solution)/shard_map/all_to_all | solution.py:83
  196.4 83.3 %all-to-all-start.1 = ((f32[8,5,128,8,32]{2,4,3,1,0:T(8,128)}), f32[8,5,128,8,32]{2,4,3,1,0:T(8,128)}, u32[]{:S(2)}, u32[]{:S(2)}) async-start(f32[8,5,128,8,32]{2,4,3,1,0:T(8,128)} %fusion.40), calls=%async_computation.1 | async-start | bytes 10485760 | tf_op jit(solution)/shard_map/all_to_all | solution.py:78
  279.8 117.3 %all-to-all-start.3 = ((f32[5,128,128,16]{1,3,0,2:T(8,128)}), f32[5,128,128,16]{1,3,0,2:T(8,128)}, u32[]{:S(2)}, u32[]{:S(2)}) async-start(f32[5,128,128,16]{1,3,0,2:T(8,128)} %copy.58), calls=%async_computation.3 | async-start | bytes 10485760 | tf_op jit(solution)/shard_map/all_to_all | solution.py:86
  291.3 66.9 %collective-permute-start.2 = (f32[5,128,2,256]{1,2,3,0:T(2,128)}, f32[5,128,2,256]{1,2,3,0:T(2,128)}, u32[]{:S(2)}, u32[]{:S(2)}) collective-permute-start(f32[5,128,2,256]{1,2,3,0:T(2,128)} %get-tuple-element.25), channel_id=1, source_target_pairs={{0,1},{1,2},{2,3},{3,4},{4,5},{5,6},{6,7},{7,8},{8,9},{9,10},{10,1... | collective-permute-start | bytes 3932168 | tf_op jit(solution)/shard_map/ppermute | solution.py:18
  292.4 90.1 %collective-permute-start.3 = (f32[5,128,2,256]{1,2,3,0:T(2,128)}, f32[5,128,2,256]{1,2,3,0:T(2,128)}, u32[]{:S(2)}, u32[]{:S(2)}) collective-permute-start(f32[5,128,2,256]{1,2,3,0:T(2,128)} %get-tuple-element.26), channel_id=1, source_target_pairs={{1,0},{2,1},{3,2},{4,3},{5,4},{6,5},{7,6},{8,7},{9,8},{10,9},{11,1... | collective-permute-start | bytes 3932168 | tf_op jit(solution)/shard_map/ppermute | solution.py:20
  301.4 16.4 %collective-permute-start.1 = (f32[5,2,8,256]{3,2,1,0:T(8,128)S(1)}, f32[5,2,8,256]{3,2,1,0:T(8,128)S(1)}, u32[]{:S(2)}, u32[]{:S(2)}) collective-permute-start(f32[5,2,8,256]{3,2,1,0:T(8,128)S(1)} %copy.64), channel_id=1, source_target_pairs={{16,0},{32,16},{48,32},{64,48},{80,64},{96,80},{112,96},{17,1},{33... | collective-permute-start | bytes 245768 | tf_op jit(solution)/shard_map/ppermute | solution.py:20
  306.9 7.0 %collective-permute-start = (f32[5,2,8,256]{3,2,1,0:T(8,128)S(1)}, f32[5,2,8,256]{3,2,1,0:T(8,128)}, u32[]{:S(2)}, u32[]{:S(2)}) collective-permute-start(f32[5,2,8,256]{3,2,1,0:T(8,128)S(1)} %copy.62), channel_id=1, source_target_pairs={{0,16},{16,32},{32,48},{48,64},{64,80},{80,96},{96,112},{1,17},{17... | collective-permute-start | bytes 245768 | tf_op jit(solution)/shard_map/ppermute | solution.py:18
  321.0 61.6 %copy-start.3 = (f32[128,8,256]{0,1,2:T(8,128)S(1)}, f32[128,8,256]{0,1,2:T(8,128)}, u32[]{:S(2)}) copy-start(f32[128,8,256]{0,1,2:T(8,128)} %copy.37) | copy-start | bytes 3145732
  321.0 61.6 %copy-start.6 = (f32[128,8,256]{0,1,2:T(8,128)S(1)}, f32[128,8,256]{0,1,2:T(8,128)}, u32[]{:S(2)}) copy-start(f32[128,8,256]{0,1,2:T(8,128)} %copy.38) | copy-start | bytes 3145732
  397.1 5.6 %copy-start.4 = (f32[128,8,256]{0,1,2:T(8,128)S(1)}, f32[128,8,256]{0,1,2:T(8,128)}, u32[]{:S(2)}) copy-start(f32[128,8,256]{0,1,2:T(8,128)} %copy.37) | copy-start | bytes 3145732
  441.2 3.2 slice-start
  444.4 7.7 %copy-start.1 = (f32[128,128]{1,0:T(8,128)S(1)}, f32[128,128]{1,0:T(8,128)}, u32[]{:S(2)}) copy-start(f32[128,128]{1,0:T(8,128)} %param.10) | copy-start | bytes 196612
